TPU v7x, 32 devices: a whole 2x2x4 slice. The times are simulated.
32 devices in a mesh: replica: 4 (over y, core), kvhead: 4 (over z), ffn: 2 (over x).
Axes of the slice: x: 2, y: 2, z: 4, core: 2. Of those that a mesh axis runs over, the one named last changes fastest.
Arguments:
- queries: bfloat16 [16, 16384], P('replica', 'kvhead'), may hold values from -400 to 400
- k_cache: bfloat16 [512, 64, 1024], P(('replica', 'ffn'), None, 'kvhead'), may hold values from -6 to 6
- v_cache: bfloat16 [512, 64, 1024], P(('replica', 'ffn'), None, 'kvhead'), may hold values from -6 to 6
- page_table: int32 [16, 32], P('replica', 'ffn'), may hold values from 0 to 63, as said below
- seq_lens: int32 [16], P('replica'), may hold values from 1 to 2048, as said below
- out_proj: bfloat16 [16384, 16384], P('kvhead', ('replica', 'ffn')), may hold values from -0.125 to 0.125
- residual: bfloat16 [16, 16384], P('kvhead', ('replica', 'ffn')), may hold values from -40 to 40
- norm_gain: bfloat16 [16384], P(('replica', 'ffn')), may hold values from 0.099609375 to 1.8984375
- gate_weight: bfloat16 [26624, 16384], P(('replica', 'kvhead', 'ffn')), may hold values from -0.046875 to 0.046875
- up_weight: bfloat16 [26624, 16384], P(('replica', 'kvhead', 'ffn')), may hold values from -0.046875 to 0.046875
Outputs:
- post_attn: bfloat16 [16, 16384], P('kvhead', ('replica', 'ffn'))
- hidden: bfloat16 [16, 26624], P(None, ('replica', 'kvhead', 'ffn'))
Inputs may be any that keep to these rules, and one draw needn't show every extreme that they name: `page_table`: over the 4 rows of one replica, the entries of page columns j with the same j // 16 name every pool page 0 to 63 exactly once. `seq_lens`: some row has length 2048.
All inputs are finite; a program needn't handle non-finite values.
Results may differ from a plain program's by a relative error of at most 0.0079.
Values may be sent and summed in bfloat16 or wider, within the bound.
A program may use at most 192 MiB of HBM per device.

v0:
```python
import math
import jax
import jax.numpy as jnp
from jax import lax
from jax.sharding import PartitionSpec as P

D = 16384
HD = 128
GQ = 16
NEG_FILL = -1e30
NORM_EPS = 1e-05


def merged(part, axis, combine):
    gathered = jax.tree.map(lambda a: lax.all_gather(a, axis), part)

    def take(source):
        return jax.tree.map(lambda a: lax.dynamic_index_in_dim(a, source, 0, False), gathered)

    return lax.fori_loop(
        1, lax.axis_size(axis), lambda source, state: combine(state, take(source)), take(0)
    )


def join_parts(earlier, later):
    first_max, first_total, first_out = earlier
    second_max, second_total, second_out = later
    overall = jnp.maximum(first_max, second_max)
    first_factor = jnp.exp(first_max - overall)
    second_factor = jnp.exp(second_max - overall)
    joined_total = first_total * first_factor + second_total * second_factor
    joined_out = first_out * first_factor[..., None] + second_out * second_factor[..., None]
    return (overall, joined_total, joined_out)


def per_device(
    queries,
    k_cache,
    v_cache,
    page_table,
    seq_lens,
    out_proj,
    residual,
    norm_gain,
    gate_weight,
    up_weight,
):
    score_scale = 1.0 / math.sqrt(HD)
    row_count = queries.shape[0]
    local_heads = k_cache.shape[2] // HD
    span_len = page_table.shape[1] * k_cache.shape[1]
    key_rows = k_cache[page_table].reshape(row_count, span_len, local_heads, HD)
    value_rows = v_cache[page_table].reshape(row_count, span_len, local_heads, HD)
    query_heads = queries.reshape(row_count, local_heads, GQ, HD)
    scores = (
        jnp.einsum("rkgd,rskd->rkgs", query_heads, key_rows, preferred_element_type=jnp.float32)
        * score_scale
    )
    positions = lax.axis_index("ffn") * span_len + jnp.arange(span_len, dtype=jnp.int32)
    visible = (positions[None, :] < seq_lens[:, None])[:, None, None, :]
    block_max = jnp.max(jnp.where(visible, scores, NEG_FILL), axis=-1)
    weights = jnp.where(visible, jnp.exp(scores - block_max[..., None]), 0.0)
    block_total = jnp.sum(weights, axis=-1)
    block_out = jnp.einsum(
        "rkgs,rskd->rkgd",
        weights.astype(jnp.bfloat16),
        value_rows,
        preferred_element_type=jnp.float32,
    )
    overall, denominator, weighted = merged((block_max, block_total, block_out), "ffn", join_parts)
    contexts = (
        (weighted / denominator[..., None])
        .astype(jnp.bfloat16)
        .reshape(row_count, local_heads * GQ * HD)
    )
    partial_value = jnp.dot(
        lax.all_gather(contexts, "replica", axis=0, tiled=True),
        out_proj,
        preferred_element_type=jnp.float32,
    )
    own_count = residual.shape[0]
    own_first = lax.axis_index("kvhead") * own_count
    own_part = lax.dynamic_slice_in_dim(partial_value, own_first, own_count, 0) + residual.astype(
        jnp.float32
    )
    partial_value = lax.dynamic_update_slice_in_dim(partial_value, own_part, own_first, 0)
    gain_wide = norm_gain.astype(jnp.float32)
    summed = lax.psum(partial_value, "kvhead")
    post_all = summed.astype(jnp.bfloat16)
    post_attn = lax.dynamic_slice_in_dim(post_all, own_first, own_count, 0)
    widened = post_all.astype(jnp.float32)
    squares = lax.psum(jnp.sum(widened * widened, axis=1), ("replica", "ffn"))
    normed = (widened * lax.rsqrt(squares / D + NORM_EPS)[:, None] * gain_wide).astype(jnp.bfloat16)
    contract = (((1,), (1,)), ((), ()))
    shard_cols = lax.all_gather(normed, ("replica", "ffn"), axis=1, tiled=True)
    gate_sum = lax.dot_general(
        shard_cols, gate_weight, contract, preferred_element_type=jnp.float32
    )
    up_sum = lax.dot_general(shard_cols, up_weight, contract, preferred_element_type=jnp.float32)
    hidden = (jax.nn.silu(gate_sum) * up_sum).astype(jnp.bfloat16)
    return (post_attn, hidden)


def solution(mesh):
    in_specs = (
        P("replica", "kvhead"),
        P(("replica", "ffn"), None, "kvhead"),
        P(("replica", "ffn"), None, "kvhead"),
        P("replica", "ffn"),
        P("replica"),
        P("kvhead", ("replica", "ffn")),
        P("kvhead", ("replica", "ffn")),
        P(("replica", "ffn")),
        P(("replica", "kvhead", "ffn"), None),
        P(("replica", "kvhead", "ffn"), None),
    )
    out_specs = (P("kvhead", ("replica", "ffn")), P(None, ("replica", "kvhead", "ffn")))
    return jax.shard_map(
        per_device, mesh=mesh, in_specs=in_specs, out_specs=out_specs, check_vma=False
    )
```

profile of v0, /device:TPU:1, one launch (start us, length us, event | category | flops | bytes accessed | tf_op | source)
XLA Modules:
  0.0 121.5 jit_solution(7688263210400951377)
XLA Ops:
  0.6 0.0 copy-start
  0.7 0.9 broadcast_compare_fusion
  1.5 0.7 compare_select_fusion
  2.2 0.1 reshape.100
  2.3 0.0 copy-done
  2.3 2.0 %gather_fusion = bf16[64,64,256]{2,1,0:T(8,128)(2,1)} fusion(bf16[64,64,256]{2,1,0:T(8,128)(2,1)S(1)} %copy-done, s32[1024]{0:T(1024)S(1)} %pad_clamp_fusion), kind=kCustom, calls=%fused_computation | custom fusion | bytes 4194560 | tf_op jit(solution)/shard_map/gather | solution.py:52
  4.4 0.0 copy-start.2
  4.4 2.6 %reshape.95 = bf16[4,1024,2,128]{3,2,1,0:T(2,128)(2,1)S(1)} reshape(bf16[64,64,256]{2,1,0:T(8,128)(2,1)} %gather_fusion) | data formatting | bytes 4194304 | tf_op jit(solution)/shard_map/reshape | solution.py:52
  6.9 0.0 copy-done.2
  6.9 0.7 select_reduce_fusion
  7.7 0.3 bitcast_reduce_fusion
  7.9 3.8 %all-gather.2 = f32[8,2,16]{2,1,0:T(2,128)S(1)} all-gather(f32[4,2,16]{2,1,0:T(2,128)S(1)} %bitcast_reduce_fusion), channel_id=4, replica_groups=mesh['replica'=4,'kvhead'=4,'ffn'=2] {'ffn'}, dimensions={0}, use_global_device_ids=true | all-gather | bytes 1536 | tf_op jit(solution)/shard_map/all_gather | solution.py:15
  11.7 3.2 %all-gather.1 = f32[8,2,16]{2,1,0:T(2,128)S(1)} all-gather(f32[4,2,16]{2,1,0:T(2,128)S(1)} %get-tuple-element.21), channel_id=3, replica_groups=mesh['replica'=4,'kvhead'=4,'ffn'=2] {'ffn'}, dimensions={0}, use_global_device_ids=true | all-gather | bytes 1536 | tf_op jit(solution)/shard_map/all_gather | solution.py:15
  14.9 2.3 %gather_fusion.1 = bf16[64,64,256]{2,1,0:T(8,128)(2,1)S(1)} fusion(bf16[64,64,256]{2,1,0:T(8,128)(2,1)} %param.12, s32[1024]{0:T(1024)S(1)} %pad_clamp_fusion), kind=kCustom, calls=%fused_computation.1 | custom fusion | bytes 4194560 | tf_op jit(solution)/shard_map/gather | solution.py:53
  17.2 2.1 %reshape.97 = bf16[4,1024,2,128]{3,2,1,0:T(2,128)(2,1)} reshape(bf16[64,64,256]{2,1,0:T(8,128)(2,1)S(1)} %gather_fusion.1) | data formatting | bytes 4194304 | tf_op jit(solution)/shard_map/reshape | solution.py:53
  19.3 2.0 %fusion = f32[4,2,16,128]{3,2,1,0:T(8,128)S(1)} fusion(bf16[4,1024,2,128]{3,2,1,0:T(2,128)(2,1)} %reshape.97, f32[4,2,1024,16]{2,3,1,0:T(8,128)S(1)} %get-tuple-element.22, f32[4,2,16]{2,1,0:T(2,128)S(1)} %get-tuple-element.21, pred[4,1024]{1,0:T(4,128)(4,1)S(1)} %broadcast_compare_fusion), kind=kOutput, calls=%fused_computation.2 | convolution fusion | flops 33947648 | bytes 2691584 | tf_op jit(solution)/shard_map/rkgs,rskd->rkgd/dot_general | solution.py:64
  21.3 3.8 %all-gather = f32[8,2,16,128]{3,2,1,0:T(8,128)S(1)} all-gather(f32[4,2,16,128]{3,2,1,0:T(8,128)S(1)} %fusion), channel_id=2, replica_groups=mesh['replica'=4,'kvhead'=4,'ffn'=2] {'ffn'}, dimensions={0}, use_global_device_ids=true | all-gather | bytes 196608 | tf_op jit(solution)/shard_map/all_gather | solution.py:15
  25.1 0.1 fusion.16
  25.3 9.3 %all-gather.3 = bf16[4,4,4096]{2,1,0:T(4,128)(2,1)S(1)} all-gather(bf16[1,4,4096]{2,1,0:T(4,128)(2,1)S(1)} %reshape.139), channel_id=1, replica_groups=mesh['replica'=4,'kvhead'=4,'ffn'=2] {'replica'}, dimensions={0}, use_global_device_ids=true | all-gather | bytes 163840 | tf_op jit(solution)/shard_map/all_gather | solution.py:77
  34.6 0.0 copy-start.3
  34.6 0.0 copy-start.4
  34.6 8.1 %fusion.23 = f32[16,2048]{1,0:T(8,128)S(1)} fusion(bf16[16,4096]{1,0:T(8,128)(2,1)S(1)} %reshape.140, bf16[4096,2048]{1,0:T(8,128)(2,1)} %param.15), kind=kOutput, calls=%fused_computation.41 | convolution fusion | flops 268435456 | bytes 17039360 | tf_op jit(solution)/shard_map/dot_general | solution.py:76
  42.7 0.0 copy-done.3
  42.7 17.8 %all-reduce.1 = bf16[16,2048]{1,0:T(8,128)(2,1)S(1)} all-reduce(f32[16,2048]{1,0:T(8,128)S(1)} %add_dynamic-update-slice_fusion), channel_id=1, replica_groups=mesh['replica'=4,'kvhead'=4,'ffn'=2] {'kvhead'}, use_global_device_ids=true, to_apply=%region_2.3 | all-reduce | flops 32768 | bytes 196608 | tf_op jit(solution)/shard_map/psum | solution.py:88
  60.5 0.1 fusion.11
  60.6 17.2 %psum.15 = f32[16]{0:T(128)S(1)} all-reduce(f32[16]{0:T(128)S(1)} %fusion.11), channel_id=1, replica_groups=mesh['replica'=4,'kvhead'=4,'ffn'=2] {'replica','ffn'}, use_global_device_ids=true, to_apply=%region_4.5 | all-reduce | flops 16 | bytes 128 | tf_op jit(solution)/shard_map/psum | solution.py:92
  77.8 0.0 copy-done.4
  77.8 0.1 fusion.13
  77.9 17.4 %all_gather.31 = bf16[16,16384]{1,0:T(8,128)(2,1)S(1)} all-gather(bf16[16,2048]{1,0:T(8,128)(2,1)S(1)} %fusion.13), channel_id=1, replica_groups=mesh['replica'=4,'kvhead'=4,'ffn'=2] {'replica','ffn'}, dimensions={1}, use_global_device_ids=true | all-gather | bytes 589824 | tf_op jit(solution)/shard_map/all_gather | solution.py:95
  95.3 12.4 %fusion.24 = f32[16,832]{1,0:T(8,128)S(1)} fusion(bf16[16,16384]{1,0:T(8,128)(2,1)S(1)} %all_gather.31, bf16[832,16384]{1,0:T(8,128)(2,1)} %param.18), kind=kOutput, calls=%fused_computation.42 | convolution fusion | flops 436207616 | bytes 27840512 | tf_op jit(solution)/shard_map/dot_general | solution.py:96
  107.7 0.0 copy-start.1
  107.7 13.2 %fusion.7 = bf16[16,832]{1,0:T(8,128)(2,1)} fusion(bf16[16,16384]{1,0:T(8,128)(2,1)S(1)} %all_gather.31, bf16[832,16384]{1,0:T(8,128)(2,1)} %param.19, f32[16,832]{1,0:T(8,128)S(1)} %fusion.24), kind=kOutput, calls=%fused_computation.8 | convolution fusion | flops 436287488 | bytes 27867136 | tf_op jit(solution)/shard_map/dot_general | solution.py:99
  120.9 0.6 constant_dynamic-slice_fusion
  121.5 0.0 copy-done.1
  (9 shorter events, 0.1 us)
Async XLA Ops:
  0.6 1.7 %copy-start = (bf16[64,64,256]{2,1,0:T(8,128)(2,1)S(1)}, bf16[64,64,256]{2,1,0:T(8,128)(2,1)}, u32[]{:S(2)}) copy-start(bf16[64,64,256]{2,1,0:T(8,128)(2,1)} %param.11) | copy-start | bytes 6291460
  4.4 2.6 %copy-start.2 = (bf16[4,4096]{1,0:T(4,128)(2,1)S(1)}, bf16[4,4096]{1,0:T(4,128)(2,1)}, u32[]{:S(2)}) copy-start(bf16[4,4096]{1,0:T(4,128)(2,1)} %param.10) | copy-start | bytes 98308
  34.6 8.1 %copy-start.3 = (bf16[4,2048]{1,0:T(4,128)(2,1)S(1)}, bf16[4,2048]{1,0:T(4,128)(2,1)}, u32[]{:S(2)}) copy-start(bf16[4,2048]{1,0:T(4,128)(2,1)} %param.16) | copy-start | bytes 49156
  34.6 43.2 %copy-start.4 = (bf16[2048]{0:T(1024)(128)(2,1)S(1)}, bf16[2048]{0:T(1024)(128)(2,1)}, u32[]{:S(2)}) copy-start(bf16[2048]{0:T(1024)(128)(2,1)} %param.17) | copy-start | bytes 12292
  107.7 13.8 %copy-start.1 = (bf16[64,64,256]{2,1,0:T(8,128)(2,1)S(1)}, bf16[64,64,256]{2,1,0:T(8,128)(2,1)}, u32[]{:S(2)}) copy-start(bf16[64,64,256]{2,1,0:T(8,128)(2,1)} %param.11) | copy-start | bytes 6291460
where the time goes:
time: 122 us; the launch traced here: 121 us
  blocking collectives  72.4 us (59%)
  matrix products  36.4 us (30%)
  local copies, waits for them, and re-layouts  9.74 us (8%)
  other arithmetic  2.21 us (2%)
    psum x1, blocking collectives, per_device(): summed = lax.psum(partial_value, 'kvhead')  17.8 us
    all_gather x1, blocking collectives, per_device(): shard_cols = lax.all_gather(normed, ('replica', 'ffn'), axis=1, tiled=True)  17.4 us
    psum x1, blocking collectives, per_device(): squares = lax.psum(jnp.sum(widened * widened, axis=1), ('replica', 'ffn'))  17.2 us
    dot_general x1, matrix products, per_device(): lax.dot_general(shard_cols, up_weight, contract, preferred_element_type=j...  13.2 us
    dot_general x1, matrix products, per_device(): lax.dot_general(shard_cols, gate_weight, contract, preferred_element_type...  12.4 us
    all_gather x3, blocking collectives, merged(): gathered = jax.tree.map(lambda a: lax.all_gather(a, axis), part)  10.7 us
    all_gather x1, blocking collectives, per_device(): lax.all_gather(contexts, 'replica', axis=0, tiled=True)  9.29 us
    dot_general x1, matrix products, per_device(): jnp.dot(lax.all_gather(contexts, 'replica', axis=0, tiled=True), out_proj...  8.05 us

commit v1 on v0

--- a/solution.py
+++ b/solution.py
@@ -85,7 +85,7 @@
     )
     partial_value = lax.dynamic_update_slice_in_dim(partial_value, own_part, own_first, 0)
     gain_wide = norm_gain.astype(jnp.float32)
-    summed = lax.psum(partial_value, "kvhead")
+    summed = jnp.sum(lax.all_gather(partial_value, "kvhead"), axis=0)
     post_all = summed.astype(jnp.bfloat16)
     post_attn = lax.dynamic_slice_in_dim(post_all, own_first, own_count, 0)
     widened = post_all.astype(jnp.float32)

time: 122 us -> 117 us (0.959)
  blocking collectives: 72.4 us -> 67.2 us
    psum x1 -> x0, blocking collectives: 17.8 us -> none  [per_device(): summed = lax.psum(partial_value, 'kvhead')]
    all_gather x0 -> x1, blocking collectives: none -> 15.2 us  [per_device(): summed = jnp.sum(lax.all_gather(partial_value, 'kvhead'), axis=0)]
    psum x1, blocking collectives: 17.2 us -> 14.6 us  [per_device(): squares = lax.psum(jnp.sum(widened * widened, axis=1), ('replica', 'ffn'))]
where the time goes in v1:
time: 117 us; the launch traced here: 116 us
  blocking collectives  67.2 us (57%)
  matrix products  36.4 us (31%)
  local copies, waits for them, and re-layouts  9.75 us (8%)
  other arithmetic  2.24 us (2%)
    all_gather x1, blocking collectives, per_device(): shard_cols = lax.all_gather(normed, ('replica', 'ffn'), axis=1, tiled=True)  17.4 us
    all_gather x1, blocking collectives, per_device(): summed = jnp.sum(lax.all_gather(partial_value, 'kvhead'), axis=0)  15.2 us
    psum x1, blocking collectives, per_device(): squares = lax.psum(jnp.sum(widened * widened, axis=1), ('replica', 'ffn'))  14.6 us
    dot_general x1, matrix products, per_device(): lax.dot_general(shard_cols, up_weight, contract, preferred_element_type=j...  13.2 us
    dot_general x1, matrix products, per_device(): lax.dot_general(shard_cols, gate_weight, contract, preferred_element_type...  12.4 us
    all_gather x3, blocking collectives, merged(): gathered = jax.tree.map(lambda a: lax.all_gather(a, axis), part)  10.7 us
    all_gather x1, blocking collectives, per_device(): lax.all_gather(contexts, 'replica', axis=0, tiled=True)  9.29 us
    dot_general x1, matrix products, per_device(): jnp.dot(lax.all_gather(contexts, 'replica', axis=0, tiled=True), out_proj...  8.05 us

profile of v1, /device:TPU:1, one launch (start us, length us, event | category | flops | bytes accessed | tf_op | source)
XLA Modules:
  0.0 116.4 jit_solution(15870594650556119881)
XLA Ops:
  0.6 0.0 copy-start
  0.7 0.9 broadcast_compare_fusion
  1.5 0.7 compare_select_fusion
  2.2 0.1 reshape.102
  2.3 0.0 copy-done
  2.3 2.0 %gather_fusion = bf16[64,64,256]{2,1,0:T(8,128)(2,1)} fusion(bf16[64,64,256]{2,1,0:T(8,128)(2,1)S(1)} %copy-done, s32[1024]{0:T(1024)S(1)} %pad_clamp_fusion), kind=kCustom, calls=%fused_computation | custom fusion | bytes 4194560 | tf_op jit(solution)/shard_map/gather | solution.py:52
  4.4 0.0 copy-start.2
  4.4 2.6 %reshape.97 = bf16[4,1024,2,128]{3,2,1,0:T(2,128)(2,1)S(1)} reshape(bf16[64,64,256]{2,1,0:T(8,128)(2,1)} %gather_fusion) | data formatting | bytes 4194304 | tf_op jit(solution)/shard_map/reshape | solution.py:52
  6.9 0.0 copy-done.2
  6.9 0.7 select_reduce_fusion
  7.7 0.3 bitcast_reduce_fusion
  7.9 3.8 %all-gather.2 = f32[8,2,16]{2,1,0:T(2,128)S(1)} all-gather(f32[4,2,16]{2,1,0:T(2,128)S(1)} %bitcast_reduce_fusion), channel_id=4, replica_groups=mesh['replica'=4,'kvhead'=4,'ffn'=2] {'ffn'}, dimensions={0}, use_global_device_ids=true | all-gather | bytes 1536 | tf_op jit(solution)/shard_map/all_gather | solution.py:15
  11.7 3.2 %all-gather.1 = f32[8,2,16]{2,1,0:T(2,128)S(1)} all-gather(f32[4,2,16]{2,1,0:T(2,128)S(1)} %get-tuple-element.21), channel_id=3, replica_groups=mesh['replica'=4,'kvhead'=4,'ffn'=2] {'ffn'}, dimensions={0}, use_global_device_ids=true | all-gather | bytes 1536 | tf_op jit(solution)/shard_map/all_gather | solution.py:15
  14.9 2.3 %gather_fusion.1 = bf16[64,64,256]{2,1,0:T(8,128)(2,1)S(1)} fusion(bf16[64,64,256]{2,1,0:T(8,128)(2,1)} %param.12, s32[1024]{0:T(1024)S(1)} %pad_clamp_fusion), kind=kCustom, calls=%fused_computation.1 | custom fusion | bytes 4194560 | tf_op jit(solution)/shard_map/gather | solution.py:53
  17.2 2.1 %reshape.99 = bf16[4,1024,2,128]{3,2,1,0:T(2,128)(2,1)} reshape(bf16[64,64,256]{2,1,0:T(8,128)(2,1)S(1)} %gather_fusion.1) | data formatting | bytes 4194304 | tf_op jit(solution)/shard_map/reshape | solution.py:53
  19.3 2.0 %fusion = f32[4,2,16,128]{3,2,1,0:T(8,128)S(1)} fusion(bf16[4,1024,2,128]{3,2,1,0:T(2,128)(2,1)} %reshape.99, f32[4,2,1024,16]{2,3,1,0:T(8,128)S(1)} %get-tuple-element.22, f32[4,2,16]{2,1,0:T(2,128)S(1)} %get-tuple-element.21, pred[4,1024]{1,0:T(4,128)(4,1)S(1)} %broadcast_compare_fusion), kind=kOutput, calls=%fused_computation.2 | convolution fusion | flops 33947648 | bytes 2691584 | tf_op jit(solution)/shard_map/rkgs,rskd->rkgd/dot_general | solution.py:64
  21.3 3.8 %all-gather = f32[8,2,16,128]{3,2,1,0:T(8,128)S(1)} all-gather(f32[4,2,16,128]{3,2,1,0:T(8,128)S(1)} %fusion), channel_id=2, replica_groups=mesh['replica'=4,'kvhead'=4,'ffn'=2] {'ffn'}, dimensions={0}, use_global_device_ids=true | all-gather | bytes 196608 | tf_op jit(solution)/shard_map/all_gather | solution.py:15
  25.1 0.1 fusion.16
  25.3 9.3 %all-gather.3 = bf16[4,4,4096]{2,1,0:T(4,128)(2,1)S(1)} all-gather(bf16[1,4,4096]{2,1,0:T(4,128)(2,1)S(1)} %reshape.141), channel_id=1, replica_groups=mesh['replica'=4,'kvhead'=4,'ffn'=2] {'replica'}, dimensions={0}, use_global_device_ids=true | all-gather | bytes 163840 | tf_op jit(solution)/shard_map/all_gather | solution.py:77
  34.6 0.0 copy-start.3
  34.6 0.0 copy-start.4
  34.6 8.1 %fusion.23 = f32[16,2048]{1,0:T(8,128)S(1)} fusion(bf16[16,4096]{1,0:T(8,128)(2,1)S(1)} %reshape.142, bf16[4096,2048]{1,0:T(8,128)(2,1)} %param.15), kind=kOutput, calls=%fused_computation.41 | convolution fusion | flops 268435456 | bytes 17039360 | tf_op jit(solution)/shard_map/dot_general | solution.py:76
  42.7 0.0 copy-done.3
  42.7 15.2 %all_gather.41 = f32[4,16,2048]{2,1,0:T(8,128)S(1)} all-gather(f32[1,16,2048]{2,1,0:T(8,128)S(1)} %bitcast_dynamic-update-slice_fusion), channel_id=1, replica_groups=mesh['replica'=4,'kvhead'=4,'ffn'=2] {'kvhead'}, dimensions={0}, use_global_device_ids=true | all-gather | bytes 655360 | tf_op jit(solution)/shard_map/all_gather | solution.py:88
  58.0 0.1 fusion.11
  58.1 14.6 %psum.7 = f32[16]{0:T(128)S(1)} all-reduce(f32[16]{0:T(128)S(1)} %fusion.11), channel_id=1, replica_groups=mesh['replica'=4,'kvhead'=4,'ffn'=2] {'replica','ffn'}, use_global_device_ids=true, to_apply=%region_4.5 | all-reduce | flops 16 | bytes 128 | tf_op jit(solution)/shard_map/psum | solution.py:92
  72.7 0.0 copy-done.4
  72.7 0.1 fusion.13
  72.7 17.4 %all_gather.42 = bf16[16,16384]{1,0:T(8,128)(2,1)S(1)} all-gather(bf16[16,2048]{1,0:T(8,128)(2,1)S(1)} %fusion.13), channel_id=1, replica_groups=mesh['replica'=4,'kvhead'=4,'ffn'=2] {'replica','ffn'}, dimensions={1}, use_global_device_ids=true | all-gather | bytes 589824 | tf_op jit(solution)/shard_map/all_gather | solution.py:95
  90.2 12.4 %fusion.24 = f32[16,832]{1,0:T(8,128)S(1)} fusion(bf16[16,16384]{1,0:T(8,128)(2,1)S(1)} %all_gather.42, bf16[832,16384]{1,0:T(8,128)(2,1)} %param.18), kind=kOutput, calls=%fused_computation.42 | convolution fusion | flops 436207616 | bytes 27840512 | tf_op jit(solution)/shard_map/dot_general | solution.py:96
  102.6 0.0 copy-start.1
  102.6 13.2 %fusion.7 = bf16[16,832]{1,0:T(8,128)(2,1)} fusion(bf16[16,16384]{1,0:T(8,128)(2,1)S(1)} %all_gather.42, bf16[832,16384]{1,0:T(8,128)(2,1)} %param.19, f32[16,832]{1,0:T(8,128)S(1)} %fusion.24), kind=kOutput, calls=%fused_computation.8 | convolution fusion | flops 436287488 | bytes 27867136 | tf_op jit(solution)/shard_map/dot_general | solution.py:99
  115.7 0.6 constant_dynamic-slice_fusion
  116.4 0.0 copy-done.1
  (11 shorter events, 0.2 us)
Async XLA Ops:
  0.6 1.7 %copy-start = (bf16[64,64,256]{2,1,0:T(8,128)(2,1)S(1)}, bf16[64,64,256]{2,1,0:T(8,128)(2,1)}, u32[]{:S(2)}) copy-start(bf16[64,64,256]{2,1,0:T(8,128)(2,1)} %param.11) | copy-start | bytes 6291460
  4.4 2.6 %copy-start.2 = (bf16[4,4096]{1,0:T(4,128)(2,1)S(1)}, bf16[4,4096]{1,0:T(4,128)(2,1)}, u32[]{:S(2)}) copy-start(bf16[4,4096]{1,0:T(4,128)(2,1)} %param.10) | copy-start | bytes 98308
  34.6 8.1 %copy-start.3 = (bf16[4,2048]{1,0:T(4,128)(2,1)S(1)}, bf16[4,2048]{1,0:T(4,128)(2,1)}, u32[]{:S(2)}) copy-start(bf16[4,2048]{1,0:T(4,128)(2,1)} %param.16) | copy-start | bytes 49156
  34.6 38.1 %copy-start.4 = (bf16[2048]{0:T(1024)(128)(2,1)S(1)}, bf16[2048]{0:T(1024)(128)(2,1)}, u32[]{:S(2)}) copy-start(bf16[2048]{0:T(1024)(128)(2,1)} %param.17) | copy-start | bytes 12292
  102.6 13.8 %copy-start.1 = (bf16[64,64,256]{2,1,0:T(8,128)(2,1)S(1)}, bf16[64,64,256]{2,1,0:T(8,128)(2,1)}, u32[]{:S(2)}) copy-start(bf16[64,64,256]{2,1,0:T(8,128)(2,1)} %param.11) | copy-start | bytes 6291460
